TPU v7x, 32 devices: a whole 2x2x4 slice. The times are simulated.
32 devices in a mesh: tm: 16 (over z, y, x), atom: 2 (over core).
Axes of the slice: x: 2, y: 2, z: 4, core: 2. Of those that a mesh axis runs over, the one named last changes fastest.
Arguments:
- positions: int32 [3, 512, 512], P(None, 'tm', 'atom'), may hold values from 0 to 16383, as said below
- velocities: float32 [3, 512, 512], P(None, 'tm', 'atom'), may hold values from -6 to 6
- species: int32 [512], P('atom'), may hold values 0 or 1
- wave_vectors: int32 [3, 256], replicated, may hold values from -64 to 64
Outputs:
- isf: float32 [6, 256, 256], P(None, 'tm', 'atom')
Inputs may be any that keep to these rules, and one draw needn't show every extreme that they name: `positions`: coordinates are fixed-point fractions of the periodic box in units of 1/16384.
All inputs are finite; a program needn't handle non-finite values. No bound on the sum of `species` on one device may be relied on, other than what follows from the above.
Results may differ from a plain program's by a relative error of at most 0.0003.
Values sent between devices are 32-bit elements; how exact they have to be, the bound alone decides.
A program may use at most 64 MiB of HBM per device.

v0:
```python
import math

import jax
import jax.numpy as jnp
from jax import lax
from jax.sharding import PartitionSpec as P

WAVE_MAX = 64


highest = lax.Precision.HIGHEST


def frame_block(pos_block, vel_block, species_onehot, wave_vectors):
    summed = (
        pos_block[0][:, :, None] * wave_vectors[0]
        + pos_block[1][:, :, None] * wave_vectors[1]
        + pos_block[2][:, :, None] * wave_vectors[2]
    )
    angle_unit = jnp.float32(2.0 * math.pi / 16384.0)
    phase = jnp.remainder(summed, 16384).astype(jnp.float32) * angle_unit
    kinds = jnp.concatenate([jnp.ones_like(vel_block[:1]), vel_block], 0)
    weights = kinds[:, None] * species_onehot[None, :, None, :]
    cos_part = jnp.einsum("qsba,bak->qsbk", weights, jnp.cos(phase), precision=highest)
    sin_part = jnp.einsum("qsba,bak->qsbk", weights, jnp.sin(phase), precision=highest)
    return jnp.stack([cos_part, sin_part])


def pair_terms(cos_rows, sin_rows):
    cos_a = cos_rows[:, :, 0]
    cos_b = cos_rows[:, :, 1]
    sin_a = sin_rows[:, :, 0]
    sin_b = sin_rows[:, :, 1]
    real_part = jnp.stack(
        [
            cos_a * cos_a + sin_a * sin_a,
            cos_a * cos_b + sin_a * sin_b,
            cos_b * cos_b + sin_b * sin_b,
        ],
        2,
    ).sum(0)
    imag_part = jnp.stack(
        [
            cos_a * sin_a - sin_a * cos_a,
            cos_a * sin_b - sin_a * cos_b,
            cos_b * sin_b - sin_b * cos_b,
        ],
        2,
    ).sum(0)
    return (real_part, imag_part)


def correlate(signals, atom_total):
    frame_total = signals.shape[-1]
    waves_here = signals.shape[3]
    signal_rows = signals.reshape(-1, frame_total)
    groups = lax.axis_size("atom")
    freq_count = frame_total // groups
    lag_count = frame_total // 2 // groups
    my_index = lax.axis_index("atom")
    freq_index = my_index * freq_count + jnp.arange(freq_count, dtype=jnp.int32)
    time_index = jnp.arange(frame_total, dtype=jnp.int32)
    angle_step = jnp.float32(math.pi / frame_total)
    turns = jnp.remainder(time_index[:, None] * freq_index[None, :], 2 * frame_total)
    angles = turns.astype(jnp.float32) * angle_step
    spec_cos = jnp.dot(signal_rows, jnp.cos(angles), precision=highest).reshape(
        2, 2, 2, waves_here, freq_count
    )
    spec_sin = jnp.dot(signal_rows, jnp.sin(angles), precision=highest).reshape(
        2, 2, 2, waves_here, freq_count
    )
    real_part, imag_part = pair_terms(spec_cos, spec_sin)
    spectral_weight = jnp.where(freq_index == 0, 1.0, 2.0).astype(jnp.float32)
    real_rows = (real_part * spectral_weight).reshape(6 * waves_here, freq_count)
    imag_rows = (imag_part * spectral_weight).reshape(6 * waves_here, freq_count)
    alternating = jnp.where(time_index % 2 == 0, 1.0, -1.0).astype(jnp.float32)
    nyquist = jnp.dot(signal_rows, alternating, precision=highest).reshape(2, 2, 2, waves_here)
    nyq_a = nyquist[:, :, 0]
    nyq_b = nyquist[:, :, 1]
    nyq_real = (
        jnp.stack([nyq_a * nyq_a, nyq_a * nyq_b, nyq_b * nyq_b], 2).sum(0).reshape(6 * waves_here)
    )
    nyq_here = nyq_real * jnp.where(my_index == 0, 1.0, 0.0).astype(jnp.float32)
    lag_index = jnp.arange(lag_count * lax.axis_size("atom"), dtype=jnp.int32)
    lag_turns = jnp.remainder(lag_index[:, None] * freq_index[None, :], 2 * frame_total)
    lag_angles = lag_turns.astype(jnp.float32) * angle_step
    term = jnp.dot(jnp.cos(lag_angles), real_rows.T, precision=highest) - jnp.dot(
        jnp.sin(lag_angles), imag_rows.T, precision=highest
    )
    lag_sign = jnp.where(lag_index % 2 == 0, 1.0, -1.0).astype(jnp.float32)
    shared = lax.psum_scatter(
        term + lag_sign[:, None] * nyq_here[None, :], "atom", scatter_dimension=0, tiled=True
    )
    lag_index = my_index * lag_count + jnp.arange(lag_count, dtype=jnp.int32)
    scaled = shared / jnp.float32(2 * frame_total)
    isf = (
        scaled / (jnp.float32(atom_total) * (frame_total - lag_index).astype(jnp.float32))[:, None]
    )
    return isf.T.reshape(6, waves_here, lag_count)


def per_device(positions, velocities, species, wave_vectors):
    atom_count = positions.shape[2]
    frame_count = positions.shape[1]
    wave_count = wave_vectors.shape[1]
    block_size = math.gcd(frame_count, 2)
    block_count = frame_count // block_size
    species_onehot = jnp.stack([1 - species, species]).astype(jnp.float32)
    pos_blocks = positions.reshape(3, block_count, block_size, atom_count).transpose(1, 0, 2, 3)
    vel_blocks = velocities.reshape(3, block_count, block_size, atom_count).transpose(1, 0, 2, 3)
    raw_modes = lax.map(
        lambda operands: frame_block(operands[0], operands[1], species_onehot, wave_vectors),
        (pos_blocks, vel_blocks),
    )
    raw_modes = raw_modes.transpose(1, 2, 3, 0, 4, 5).reshape(2, 4, 2, frame_count, wave_count)
    wave_scaled = wave_vectors.astype(jnp.float32) / WAVE_MAX
    current = (
        wave_scaled[0] * raw_modes[:, 1]
        + wave_scaled[1] * raw_modes[:, 2]
        + wave_scaled[2] * raw_modes[:, 3]
    )
    modes = jnp.stack([raw_modes[:, 0], current], 1)
    atom_groups = lax.axis_size("atom")
    summed = lax.psum(modes, "atom")
    owned = lax.all_to_all(summed, "tm", split_axis=4, concat_axis=3, tiled=True)
    signals = jnp.moveaxis(owned, 3, 4)
    return correlate(signals, atom_count * atom_groups)


def solution(mesh):
    return jax.shard_map(
        per_device,
        mesh=mesh,
        in_specs=(P(None, "tm", "atom"), P(None, "tm", "atom"), P("atom"), P()),
        out_specs=P(None, "tm", "atom"),
        check_vma=False,
    )
```

profile of v0, /device:TPU:0, one launch (start us, length us, event | category | flops | bytes accessed | tf_op | source)
XLA Modules:
  0.0 160.4 jit_solution(9982431130612515028)
XLA Ops:
  9.6 81.0 %while.12 = (s32[]{:T(128)}, f32[16,2,4,2,2,256]{5,2,3,4,1,0:T(4,128)S(1)}, s32[16,3,2,256]{3,2,0,1:T(2,128)S(1)}, s32[3,256]{1,0:T(4,128)S(1)}, f32[16,3,2,256]...) while((s32[]{:T(128)}, f32[16,2,4,2,2,256]{5,2,3,4,1,0:T(4,128)S(1)}, ...), condition=%wide.region_1.2_spmd, body=%wide.region_0.1_spmd.sunk | while | flops 29900800 | bytes 194661 | solution.py:111
  9.7 2.5 %convolution_bitcast_fusion.5 = f32[1,4,2,2,256]{4,1,2,3,0:T(4,128)S(1)} fusion(s32[256]{0:T(256)S(1)} %bitcast.119, s32[2,256]{1,0:T(2,128)S(1)} %get-tuple-element.188, s32[256]{0:T(256)S(1)} %bitcast.121, s32[2,256]{1,0:T(2,128)S(1)} %get-tuple-element.190, s32[256]{0:T(256)S(1)} %bitcast.117, s32[2,256]{1,0:T(2,128)S(1)} %get-tuple-element.192, ...), kind=kOutput, calls=%fused_computation.1.clone.1 | convolution fusion | flops 14946304 | bytes 35840 | tf_op jit(solution)/shard_map/while/body/eval_jaxpr/qsba,bak->qsbk/dot_general | solution.py:24
  12.1 2.5 %convolution_bitcast_fusion.4 = f32[1,4,2,2,256]{4,1,2,3,0:T(4,128)S(1)} fusion(s32[256]{0:T(256)S(1)} %bitcast.120, s32[2,256]{1,0:T(2,128)S(1)} %get-tuple-element.188, s32[256]{0:T(256)S(1)} %bitcast.122, s32[2,256]{1,0:T(2,128)S(1)} %get-tuple-element.190, s32[256]{0:T(256)S(1)} %bitcast.118, s32[2,256]{1,0:T(2,128)S(1)} %get-tuple-element.192, ...), kind=kOutput, calls=%fused_computation.clone.1 | convolution fusion | flops 14946304 | bytes 35840 | tf_op jit(solution)/shard_map/while/body/eval_jaxpr/qsba,bak->qsbk/dot_general | solution.py:25
  14.7 2.5 %convolution_bitcast_fusion.5 = f32[1,4,2,2,256]{4,1,2,3,0:T(4,128)S(1)} fusion(s32[256]{0:T(256)S(1)} %bitcast.119, s32[2,256]{1,0:T(2,128)S(1)} %get-tuple-element.188, s32[256]{0:T(256)S(1)} %bitcast.121, s32[2,256]{1,0:T(2,128)S(1)} %get-tuple-element.190, s32[256]{0:T(256)S(1)} %bitcast.117, s32[2,256]{1,0:T(2,128)S(1)} %get-tuple-element.192, ...), kind=kOutput, calls=%fused_computation.1.clone.1 | convolution fusion | flops 14946304 | bytes 35840 | tf_op jit(solution)/shard_map/while/body/eval_jaxpr/qsba,bak->qsbk/dot_general | solution.py:24
  17.2 2.5 %convolution_bitcast_fusion.4 = f32[1,4,2,2,256]{4,1,2,3,0:T(4,128)S(1)} fusion(s32[256]{0:T(256)S(1)} %bitcast.120, s32[2,256]{1,0:T(2,128)S(1)} %get-tuple-element.188, s32[256]{0:T(256)S(1)} %bitcast.122, s32[2,256]{1,0:T(2,128)S(1)} %get-tuple-element.190, s32[256]{0:T(256)S(1)} %bitcast.118, s32[2,256]{1,0:T(2,128)S(1)} %get-tuple-element.192, ...), kind=kOutput, calls=%fused_computation.clone.1 | convolution fusion | flops 14946304 | bytes 35840 | tf_op jit(solution)/shard_map/while/body/eval_jaxpr/qsba,bak->qsbk/dot_general | solution.py:25
  19.8 2.5 %convolution_bitcast_fusion.5 = f32[1,4,2,2,256]{4,1,2,3,0:T(4,128)S(1)} fusion(s32[256]{0:T(256)S(1)} %bitcast.119, s32[2,256]{1,0:T(2,128)S(1)} %get-tuple-element.188, s32[256]{0:T(256)S(1)} %bitcast.121, s32[2,256]{1,0:T(2,128)S(1)} %get-tuple-element.190, s32[256]{0:T(256)S(1)} %bitcast.117, s32[2,256]{1,0:T(2,128)S(1)} %get-tuple-element.192, ...), kind=kOutput, calls=%fused_computation.1.clone.1 | convolution fusion | flops 14946304 | bytes 35840 | tf_op jit(solution)/shard_map/while/body/eval_jaxpr/qsba,bak->qsbk/dot_general | solution.py:24
  22.2 2.5 %convolution_bitcast_fusion.4 = f32[1,4,2,2,256]{4,1,2,3,0:T(4,128)S(1)} fusion(s32[256]{0:T(256)S(1)} %bitcast.120, s32[2,256]{1,0:T(2,128)S(1)} %get-tuple-element.188, s32[256]{0:T(256)S(1)} %bitcast.122, s32[2,256]{1,0:T(2,128)S(1)} %get-tuple-element.190, s32[256]{0:T(256)S(1)} %bitcast.118, s32[2,256]{1,0:T(2,128)S(1)} %get-tuple-element.192, ...), kind=kOutput, calls=%fused_computation.clone.1 | convolution fusion | flops 14946304 | bytes 35840 | tf_op jit(solution)/shard_map/while/body/eval_jaxpr/qsba,bak->qsbk/dot_general | solution.py:25
  24.9 2.5 %convolution_bitcast_fusion.5 = f32[1,4,2,2,256]{4,1,2,3,0:T(4,128)S(1)} fusion(s32[256]{0:T(256)S(1)} %bitcast.119, s32[2,256]{1,0:T(2,128)S(1)} %get-tuple-element.188, s32[256]{0:T(256)S(1)} %bitcast.121, s32[2,256]{1,0:T(2,128)S(1)} %get-tuple-element.190, s32[256]{0:T(256)S(1)} %bitcast.117, s32[2,256]{1,0:T(2,128)S(1)} %get-tuple-element.192, ...), kind=kOutput, calls=%fused_computation.1.clone.1 | convolution fusion | flops 14946304 | bytes 35840 | tf_op jit(solution)/shard_map/while/body/eval_jaxpr/qsba,bak->qsbk/dot_general | solution.py:24
  27.3 2.5 %convolution_bitcast_fusion.4 = f32[1,4,2,2,256]{4,1,2,3,0:T(4,128)S(1)} fusion(s32[256]{0:T(256)S(1)} %bitcast.120, s32[2,256]{1,0:T(2,128)S(1)} %get-tuple-element.188, s32[256]{0:T(256)S(1)} %bitcast.122, s32[2,256]{1,0:T(2,128)S(1)} %get-tuple-element.190, s32[256]{0:T(256)S(1)} %bitcast.118, s32[2,256]{1,0:T(2,128)S(1)} %get-tuple-element.192, ...), kind=kOutput, calls=%fused_computation.clone.1 | convolution fusion | flops 14946304 | bytes 35840 | tf_op jit(solution)/shard_map/while/body/eval_jaxpr/qsba,bak->qsbk/dot_general | solution.py:25
  29.9 2.5 %convolution_bitcast_fusion.5 = f32[1,4,2,2,256]{4,1,2,3,0:T(4,128)S(1)} fusion(s32[256]{0:T(256)S(1)} %bitcast.119, s32[2,256]{1,0:T(2,128)S(1)} %get-tuple-element.188, s32[256]{0:T(256)S(1)} %bitcast.121, s32[2,256]{1,0:T(2,128)S(1)} %get-tuple-element.190, s32[256]{0:T(256)S(1)} %bitcast.117, s32[2,256]{1,0:T(2,128)S(1)} %get-tuple-element.192, ...), kind=kOutput, calls=%fused_computation.1.clone.1 | convolution fusion | flops 14946304 | bytes 35840 | tf_op jit(solution)/shard_map/while/body/eval_jaxpr/qsba,bak->qsbk/dot_general | solution.py:24
  32.4 2.5 %convolution_bitcast_fusion.4 = f32[1,4,2,2,256]{4,1,2,3,0:T(4,128)S(1)} fusion(s32[256]{0:T(256)S(1)} %bitcast.120, s32[2,256]{1,0:T(2,128)S(1)} %get-tuple-element.188, s32[256]{0:T(256)S(1)} %bitcast.122, s32[2,256]{1,0:T(2,128)S(1)} %get-tuple-element.190, s32[256]{0:T(256)S(1)} %bitcast.118, s32[2,256]{1,0:T(2,128)S(1)} %get-tuple-element.192, ...), kind=kOutput, calls=%fused_computation.clone.1 | convolution fusion | flops 14946304 | bytes 35840 | tf_op jit(solution)/shard_map/while/body/eval_jaxpr/qsba,bak->qsbk/dot_general | solution.py:25
  35.0 2.5 %convolution_bitcast_fusion.5 = f32[1,4,2,2,256]{4,1,2,3,0:T(4,128)S(1)} fusion(s32[256]{0:T(256)S(1)} %bitcast.119, s32[2,256]{1,0:T(2,128)S(1)} %get-tuple-element.188, s32[256]{0:T(256)S(1)} %bitcast.121, s32[2,256]{1,0:T(2,128)S(1)} %get-tuple-element.190, s32[256]{0:T(256)S(1)} %bitcast.117, s32[2,256]{1,0:T(2,128)S(1)} %get-tuple-element.192, ...), kind=kOutput, calls=%fused_computation.1.clone.1 | convolution fusion | flops 14946304 | bytes 35840 | tf_op jit(solution)/shard_map/while/body/eval_jaxpr/qsba,bak->qsbk/dot_general | solution.py:24
  37.4 2.5 %convolution_bitcast_fusion.4 = f32[1,4,2,2,256]{4,1,2,3,0:T(4,128)S(1)} fusion(s32[256]{0:T(256)S(1)} %bitcast.120, s32[2,256]{1,0:T(2,128)S(1)} %get-tuple-element.188, s32[256]{0:T(256)S(1)} %bitcast.122, s32[2,256]{1,0:T(2,128)S(1)} %get-tuple-element.190, s32[256]{0:T(256)S(1)} %bitcast.118, s32[2,256]{1,0:T(2,128)S(1)} %get-tuple-element.192, ...), kind=kOutput, calls=%fused_computation.clone.1 | convolution fusion | flops 14946304 | bytes 35840 | tf_op jit(solution)/shard_map/while/body/eval_jaxpr/qsba,bak->qsbk/dot_general | solution.py:25
  40.1 2.5 %convolution_bitcast_fusion.5 = f32[1,4,2,2,256]{4,1,2,3,0:T(4,128)S(1)} fusion(s32[256]{0:T(256)S(1)} %bitcast.119, s32[2,256]{1,0:T(2,128)S(1)} %get-tuple-element.188, s32[256]{0:T(256)S(1)} %bitcast.121, s32[2,256]{1,0:T(2,128)S(1)} %get-tuple-element.190, s32[256]{0:T(256)S(1)} %bitcast.117, s32[2,256]{1,0:T(2,128)S(1)} %get-tuple-element.192, ...), kind=kOutput, calls=%fused_computation.1.clone.1 | convolution fusion | flops 14946304 | bytes 35840 | tf_op jit(solution)/shard_map/while/body/eval_jaxpr/qsba,bak->qsbk/dot_general | solution.py:24
  42.5 2.5 %convolution_bitcast_fusion.4 = f32[1,4,2,2,256]{4,1,2,3,0:T(4,128)S(1)} fusion(s32[256]{0:T(256)S(1)} %bitcast.120, s32[2,256]{1,0:T(2,128)S(1)} %get-tuple-element.188, s32[256]{0:T(256)S(1)} %bitcast.122, s32[2,256]{1,0:T(2,128)S(1)} %get-tuple-element.190, s32[256]{0:T(256)S(1)} %bitcast.118, s32[2,256]{1,0:T(2,128)S(1)} %get-tuple-element.192, ...), kind=kOutput, calls=%fused_computation.clone.1 | convolution fusion | flops 14946304 | bytes 35840 | tf_op jit(solution)/shard_map/while/body/eval_jaxpr/qsba,bak->qsbk/dot_general | solution.py:25
  47.6 2.5 %convolution_bitcast_fusion.4 = f32[1,4,2,2,256]{4,1,2,3,0:T(4,128)S(1)} fusion(s32[256]{0:T(256)S(1)} %bitcast.120, s32[2,256]{1,0:T(2,128)S(1)} %get-tuple-element.188, s32[256]{0:T(256)S(1)} %bitcast.122, s32[2,256]{1,0:T(2,128)S(1)} %get-tuple-element.190, s32[256]{0:T(256)S(1)} %bitcast.118, s32[2,256]{1,0:T(2,128)S(1)} %get-tuple-element.192, ...), kind=kOutput, calls=%fused_computation.clone.1 | convolution fusion | flops 14946304 | bytes 35840 | tf_op jit(solution)/shard_map/while/body/eval_jaxpr/qsba,bak->qsbk/dot_general | solution.py:25
  52.6 2.5 %convolution_bitcast_fusion.4 = f32[1,4,2,2,256]{4,1,2,3,0:T(4,128)S(1)} fusion(s32[256]{0:T(256)S(1)} %bitcast.120, s32[2,256]{1,0:T(2,128)S(1)} %get-tuple-element.188, s32[256]{0:T(256)S(1)} %bitcast.122, s32[2,256]{1,0:T(2,128)S(1)} %get-tuple-element.190, s32[256]{0:T(256)S(1)} %bitcast.118, s32[2,256]{1,0:T(2,128)S(1)} %get-tuple-element.192, ...), kind=kOutput, calls=%fused_computation.clone.1 | convolution fusion | flops 14946304 | bytes 35840 | tf_op jit(solution)/shard_map/while/body/eval_jaxpr/qsba,bak->qsbk/dot_general | solution.py:25
  55.3 2.5 %convolution_bitcast_fusion.5 = f32[1,4,2,2,256]{4,1,2,3,0:T(4,128)S(1)} fusion(s32[256]{0:T(256)S(1)} %bitcast.119, s32[2,256]{1,0:T(2,128)S(1)} %get-tuple-element.188, s32[256]{0:T(256)S(1)} %bitcast.121, s32[2,256]{1,0:T(2,128)S(1)} %get-tuple-element.190, s32[256]{0:T(256)S(1)} %bitcast.117, s32[2,256]{1,0:T(2,128)S(1)} %get-tuple-element.192, ...), kind=kOutput, calls=%fused_computation.1.clone.1 | convolution fusion | flops 14946304 | bytes 35840 | tf_op jit(solution)/shard_map/while/body/eval_jaxpr/qsba,bak->qsbk/dot_general | solution.py:24
  57.7 2.5 %convolution_bitcast_fusion.4 = f32[1,4,2,2,256]{4,1,2,3,0:T(4,128)S(1)} fusion(s32[256]{0:T(256)S(1)} %bitcast.120, s32[2,256]{1,0:T(2,128)S(1)} %get-tuple-element.188, s32[256]{0:T(256)S(1)} %bitcast.122, s32[2,256]{1,0:T(2,128)S(1)} %get-tuple-element.190, s32[256]{0:T(256)S(1)} %bitcast.118, s32[2,256]{1,0:T(2,128)S(1)} %get-tuple-element.192, ...), kind=kOutput, calls=%fused_computation.clone.1 | convolution fusion | flops 14946304 | bytes 35840 | tf_op jit(solution)/shard_map/while/body/eval_jaxpr/qsba,bak->qsbk/dot_general | solution.py:25
  60.3 2.5 %convolution_bitcast_fusion.5 = f32[1,4,2,2,256]{4,1,2,3,0:T(4,128)S(1)} fusion(s32[256]{0:T(256)S(1)} %bitcast.119, s32[2,256]{1,0:T(2,128)S(1)} %get-tuple-element.188, s32[256]{0:T(256)S(1)} %bitcast.121, s32[2,256]{1,0:T(2,128)S(1)} %get-tuple-element.190, s32[256]{0:T(256)S(1)} %bitcast.117, s32[2,256]{1,0:T(2,128)S(1)} %get-tuple-element.192, ...), kind=kOutput, calls=%fused_computation.1.clone.1 | convolution fusion | flops 14946304 | bytes 35840 | tf_op jit(solution)/shard_map/while/body/eval_jaxpr/qsba,bak->qsbk/dot_general | solution.py:24
  62.8 2.5 %convolution_bitcast_fusion.4 = f32[1,4,2,2,256]{4,1,2,3,0:T(4,128)S(1)} fusion(s32[256]{0:T(256)S(1)} %bitcast.120, s32[2,256]{1,0:T(2,128)S(1)} %get-tuple-element.188, s32[256]{0:T(256)S(1)} %bitcast.122, s32[2,256]{1,0:T(2,128)S(1)} %get-tuple-element.190, s32[256]{0:T(256)S(1)} %bitcast.118, s32[2,256]{1,0:T(2,128)S(1)} %get-tuple-element.192, ...), kind=kOutput, calls=%fused_computation.clone.1 | convolution fusion | flops 14946304 | bytes 35840 | tf_op jit(solution)/shard_map/while/body/eval_jaxpr/qsba,bak->qsbk/dot_general | solution.py:25
  67.8 2.5 %convolution_bitcast_fusion.4 = f32[1,4,2,2,256]{4,1,2,3,0:T(4,128)S(1)} fusion(s32[256]{0:T(256)S(1)} %bitcast.120, s32[2,256]{1,0:T(2,128)S(1)} %get-tuple-element.188, s32[256]{0:T(256)S(1)} %bitcast.122, s32[2,256]{1,0:T(2,128)S(1)} %get-tuple-element.190, s32[256]{0:T(256)S(1)} %bitcast.118, s32[2,256]{1,0:T(2,128)S(1)} %get-tuple-element.192, ...), kind=kOutput, calls=%fused_computation.clone.1 | convolution fusion | flops 14946304 | bytes 35840 | tf_op jit(solution)/shard_map/while/body/eval_jaxpr/qsba,bak->qsbk/dot_general | solution.py:25
  72.9 2.5 %convolution_bitcast_fusion.4 = f32[1,4,2,2,256]{4,1,2,3,0:T(4,128)S(1)} fusion(s32[256]{0:T(256)S(1)} %bitcast.120, s32[2,256]{1,0:T(2,128)S(1)} %get-tuple-element.188, s32[256]{0:T(256)S(1)} %bitcast.122, s32[2,256]{1,0:T(2,128)S(1)} %get-tuple-element.190, s32[256]{0:T(256)S(1)} %bitcast.118, s32[2,256]{1,0:T(2,128)S(1)} %get-tuple-element.192, ...), kind=kOutput, calls=%fused_computation.clone.1 | convolution fusion | flops 14946304 | bytes 35840 | tf_op jit(solution)/shard_map/while/body/eval_jaxpr/qsba,bak->qsbk/dot_general | solution.py:25
  75.5 2.5 %convolution_bitcast_fusion.5 = f32[1,4,2,2,256]{4,1,2,3,0:T(4,128)S(1)} fusion(s32[256]{0:T(256)S(1)} %bitcast.119, s32[2,256]{1,0:T(2,128)S(1)} %get-tuple-element.188, s32[256]{0:T(256)S(1)} %bitcast.121, s32[2,256]{1,0:T(2,128)S(1)} %get-tuple-element.190, s32[256]{0:T(256)S(1)} %bitcast.117, s32[2,256]{1,0:T(2,128)S(1)} %get-tuple-element.192, ...), kind=kOutput, calls=%fused_computation.1.clone.1 | convolution fusion | flops 14946304 | bytes 35840 | tf_op jit(solution)/shard_map/while/body/eval_jaxpr/qsba,bak->qsbk/dot_general | solution.py:24
  78.0 2.5 %convolution_bitcast_fusion.4 = f32[1,4,2,2,256]{4,1,2,3,0:T(4,128)S(1)} fusion(s32[256]{0:T(256)S(1)} %bitcast.120, s32[2,256]{1,0:T(2,128)S(1)} %get-tuple-element.188, s32[256]{0:T(256)S(1)} %bitcast.122, s32[2,256]{1,0:T(2,128)S(1)} %get-tuple-element.190, s32[256]{0:T(256)S(1)} %bitcast.118, s32[2,256]{1,0:T(2,128)S(1)} %get-tuple-element.192, ...), kind=kOutput, calls=%fused_computation.clone.1 | convolution fusion | flops 14946304 | bytes 35840 | tf_op jit(solution)/shard_map/while/body/eval_jaxpr/qsba,bak->qsbk/dot_general | solution.py:25
  80.6 2.5 %convolution_bitcast_fusion.5 = f32[1,4,2,2,256]{4,1,2,3,0:T(4,128)S(1)} fusion(s32[256]{0:T(256)S(1)} %bitcast.119, s32[2,256]{1,0:T(2,128)S(1)} %get-tuple-element.188, s32[256]{0:T(256)S(1)} %bitcast.121, s32[2,256]{1,0:T(2,128)S(1)} %get-tuple-element.190, s32[256]{0:T(256)S(1)} %bitcast.117, s32[2,256]{1,0:T(2,128)S(1)} %get-tuple-element.192, ...), kind=kOutput, calls=%fused_computation.1.clone.1 | convolution fusion | flops 14946304 | bytes 35840 | tf_op jit(solution)/shard_map/while/body/eval_jaxpr/qsba,bak->qsbk/dot_general | solution.py:24
  83.0 2.5 %convolution_bitcast_fusion.4 = f32[1,4,2,2,256]{4,1,2,3,0:T(4,128)S(1)} fusion(s32[256]{0:T(256)S(1)} %bitcast.120, s32[2,256]{1,0:T(2,128)S(1)} %get-tuple-element.188, s32[256]{0:T(256)S(1)} %bitcast.122, s32[2,256]{1,0:T(2,128)S(1)} %get-tuple-element.190, s32[256]{0:T(256)S(1)} %bitcast.118, s32[2,256]{1,0:T(2,128)S(1)} %get-tuple-element.192, ...), kind=kOutput, calls=%fused_computation.clone.1 | convolution fusion | flops 14946304 | bytes 35840 | tf_op jit(solution)/shard_map/while/body/eval_jaxpr/qsba,bak->qsbk/dot_general | solution.py:25
  88.1 2.5 %convolution_bitcast_fusion.4 = f32[1,4,2,2,256]{4,1,2,3,0:T(4,128)S(1)} fusion(s32[256]{0:T(256)S(1)} %bitcast.120, s32[2,256]{1,0:T(2,128)S(1)} %get-tuple-element.188, s32[256]{0:T(256)S(1)} %bitcast.122, s32[2,256]{1,0:T(2,128)S(1)} %get-tuple-element.190, s32[256]{0:T(256)S(1)} %bitcast.118, s32[2,256]{1,0:T(2,128)S(1)} %get-tuple-element.192, ...), kind=kOutput, calls=%fused_computation.clone.1 | convolution fusion | flops 14946304 | bytes 35840 | tf_op jit(solution)/shard_map/while/body/eval_jaxpr/qsba,bak->qsbk/dot_general | solution.py:25
  91.9 21.1 %all-reduce.3.cloned.1.call-done = f32[2,2,2,32,256]{4,2,3,1,0:T(2,128)} async-done(((f32[2,2,2,32,256]{4,2,3,1,0:T(2,128)}), f32[2,2,2,32,256]{4,2,3,1,0:T(2,128)}) %all-reduce.3.cloned.1.call-update) | async-done | bytes 262160 | tf_op jit(solution)/shard_map/psum | solution.py:124
  116.4 6.8 %all-to-all-start = ((f32[16,1,4096]{2,1,0:T(1,128)}), f32[16,1,4096]{2,1,0:T(1,128)S(1)}, u32[]{:S(2)}, u32[]{:S(2)}) async-start(f32[16,1,4096]{2,1,0:T(1,128)} %reshape.89), calls=%async_computation | async-start | bytes 524288 | tf_op jit(solution)/shard_map/all_to_all | solution.py:125
  123.5 10.0 %all-to-all-done = f32[16,1,4096]{2,1,0:T(1,128)S(1)} async-done(((f32[16,1,4096]{2,1,0:T(1,128)}), f32[16,1,4096]{2,1,0:T(1,128)S(1)}, u32[]{:S(2)}, u32[]{:S(2)}) %all-to-all-start) | async-done | bytes 262176 | tf_op jit(solution)/shard_map/all_to_all | solution.py:125
  146.5 5.6 %reduce-scatter.2.cloned.1.call-done = f32[128,96]{0,1:T(8,128)} async-done(((f32[256,96]{0,1:T(8,128)}), f32[128,96]{0,1:T(8,128)}) %reduce-scatter.2.cloned.1.call-update) | async-done | bytes 49168 | tf_op jit(solution)/shard_map/reduce_scatter | solution.py:91
  (149 shorter events, 35.5 us)
Async XLA Ops:
  6.5 106.5 %all-reduce.3.cloned.1.call-start = ((), (), s32[]{:S(2)}) async-start(), calls=%async_computation.2 | async-start | bytes 524288 | tf_op jit(solution)/shard_map/psum | solution.py:124
  7.2 1.0 copy-start
  8.2 0.7 copy-start.2
  8.9 0.7 copy-start.1
  116.4 17.1 %all-to-all-start = ((f32[16,1,4096]{2,1,0:T(1,128)}), f32[16,1,4096]{2,1,0:T(1,128)S(1)}, u32[]{:S(2)}, u32[]{:S(2)}) async-start(f32[16,1,4096]{2,1,0:T(1,128)} %reshape.89), calls=%async_computation | async-start | bytes 524288 | tf_op jit(solution)/shard_map/all_to_all | solution.py:125
  123.2 28.9 %reduce-scatter.2.cloned.1.call-start = ((), (), s32[]{:S(2)}) async-start(), calls=%async_computation.3 | async-start | bytes 147456 | tf_op jit(solution)/shard_map/reduce_scatter | solution.py:91
Sparse Core Ops, SparseCore 0:
  92.0 20.9 all-reduce.2
  146.7 5.4 reduce-scatter.1
where the time goes:
time: 161 us; the launch traced here: 160 us
  matrix products  88.1 us (55%)
  waiting for transfers between devices  36.8 us (23%)
  between operations  13.6 us (8%)
  local copies, waits for them, and re-layouts  8.99 us (6%)
  starting transfers between devices  7.01 us (4%)
  other arithmetic  4.92 us (3%)
    dot_general x16, matrix products, frame_block(): jnp.einsum('qsba,bak->qsbk', weights, jnp.sin(phase), precision=highest)  39.8 us
    dot_general x16, matrix products, frame_block(): jnp.einsum('qsba,bak->qsbk', weights, jnp.cos(phase), precision=highest)  39.3 us
    psum x1, waiting for transfers between devices, per_device(): summed = lax.psum(modes, 'atom')  21.1 us
    all_to_all x1, waiting for transfers between devices, per_device(): lax.all_to_all(summed, 'tm', split_axis=4, concat_axis=3, tiled=True)  10 us
    all_to_all x1, starting transfers between devices, per_device(): lax.all_to_all(summed, 'tm', split_axis=4, concat_axis=3, tiled=True)  6.78 us
    reduce_scatter x1, waiting for transfers between devices, correlate(): lax.psum_scatter(term + lag_sign[:, None] * nyq_here[None, :], 'atom', sc...  5.55 us
    unnamed x9, local copies, waits for them, and re-layouts  4.93 us
  transfers between devices with their start and end apart: 3, of which 3 were waited for; matrix products, arithmetic and copies ran while one was open for 0% of the time, Pallas kernels for 0%

commit v1 on v0

--- a/solution.py
+++ b/solution.py
@@ -2,7 +2,11 @@
 
 import jax
 import jax.numpy as jnp
+import ml_dtypes
+import numpy as np
 from jax import lax
+from jax.experimental import pallas as pl
+from jax.experimental.pallas import tpu as pltpu
 from jax.sharding import PartitionSpec as P
 
 WAVE_MAX = 64
@@ -99,7 +103,7 @@
     return isf.T.reshape(6, waves_here, lag_count)
 
 
-def per_device(positions, velocities, species, wave_vectors):
+def per_device_general(positions, velocities, species, wave_vectors):
     atom_count = positions.shape[2]
     frame_count = positions.shape[1]
     wave_count = wave_vectors.shape[1]
@@ -127,7 +131,336 @@
     return correlate(signals, atom_count * atom_groups)
 
 
+GROUP = 16
+STEP = 2
+
+
+def even_coeffs(func, degree):
+    fit = np.polynomial.chebyshev.Chebyshev.interpolate(
+        lambda z: func(np.sqrt(np.maximum(z, 1e-12))), degree, domain=[0.0, 0.25]
+    )
+    return [float(v) for v in fit.convert(kind=np.polynomial.Polynomial).coef]
+
+
+COS_COEFFS = even_coeffs(lambda r: np.cos(2 * np.pi * r), 5)
+SIN_COEFFS = even_coeffs(lambda r: np.sin(2 * np.pi * r) / r, 4)
+
+
+def dft_tables(frames):
+    turns = np.outer(np.arange(frames), np.arange(frames)) % (2 * frames)
+    angle = turns * (np.pi / frames)
+    sine = np.sin(angle)
+    sine[:, 0] = 1.0 - 2.0 * (np.arange(frames) % 2)
+    table = np.concatenate([np.cos(angle), sine], 1).astype(np.float32)
+    high = table.astype(ml_dtypes.bfloat16)
+    low = (table - high.astype(np.float32)).astype(ml_dtypes.bfloat16)
+    return np.stack([high, low])
+
+
+def horner(coeffs, z):
+    value = coeffs[-1] * z + coeffs[-2]
+    for coeff in coeffs[-3::-1]:
+        value = value * z + coeff
+    return value
+
+
+def split(value):
+    high = value.astype(jnp.bfloat16)
+    low = (value - high.astype(jnp.float32)).astype(jnp.bfloat16)
+    return high, low
+
+
+def dot_rows(left, right):
+    return lax.dot_general(
+        left, right, (((1,), (1,)), ((), ())), preferred_element_type=jnp.float32
+    )
+
+
+def fused_kernel(
+    tm_size,
+    pos_ref,
+    vel_ref,
+    species_ref,
+    wave_ref,
+    table_hbm,
+    out_ref,
+    table,
+    wave_cols,
+    factor,
+    weights,
+    acc,
+    modes,
+    from_pair,
+    summed,
+    signals,
+    result,
+    result_in,
+    table_sem,
+    pair_send,
+    pair_recv,
+    peer_send,
+    peer_recv,
+    last_send,
+    last_recv,
+):
+    me = lax.axis_index("tm")
+    core = lax.axis_index("atom")
+    other = 1 - core
+    frames = pos_ref.shape[1]
+    waves = wave_ref.shape[1]
+    atoms = pos_ref.shape[2]
+    groups = frames // GROUP
+    frame_total = frames * tm_size
+
+    barrier = pltpu.get_barrier_semaphore()
+    for hop in range(1, tm_size):
+        peer = lax.rem(me + hop, tm_size)
+        pl.semaphore_signal(
+            barrier, inc=1, device_id=(peer, core), device_id_type=pl.DeviceIdType.MESH
+        )
+    pl.semaphore_signal(
+        barrier, inc=1, device_id=(me, other), device_id_type=pl.DeviceIdType.MESH
+    )
+    table_copy = pltpu.make_async_copy(table_hbm, table, table_sem)
+    table_copy.start()
+
+    lane = lax.broadcasted_iota(jnp.int32, (waves, 128), 1)
+    for d in range(3):
+        row = wave_ref[d : d + 1, :].astype(jnp.float32)
+        wave_cols[d] = jnp.broadcast_to(row, (128, waves)).T
+    scaled = jnp.where(
+        lane < 64, wave_cols[0], jnp.where(lane < 96, wave_cols[1], wave_cols[2])
+    ) * (1.0 / WAVE_MAX)
+    factor[...] = jnp.where(lane < 32, 1.0, scaled)
+    species_b = species_ref[...].astype(jnp.float32)
+    species_a = 1.0 - species_b
+
+    def trig(t):
+        turn = None
+        for d in range(3):
+            coord = pos_ref[d, pl.ds(t, 1), :].astype(jnp.float32) * (1.0 / 16384.0)
+            wave = wave_cols[d]
+            term = jnp.concatenate([wave] * (atoms // 128), 1) * coord
+            turn = term if turn is None else turn + term
+        magic = jnp.float32(12582912.0)
+        rest = turn - ((turn + magic) - magic)
+        z = rest * rest
+        return horner(COS_COEFFS, z), rest * horner(SIN_COEFFS, z)
+
+    def pair_copy(tg):
+        return pltpu.make_async_remote_copy(
+            src_ref=modes.at[tg, other],
+            dst_ref=from_pair.at[tg],
+            send_sem=pair_send.at[tg],
+            recv_sem=pair_recv.at[tg],
+            device_id=(me, other),
+            device_id_type=pl.DeviceIdType.MESH,
+        )
+
+    def peer_copy(tg, hop):
+        peer = lax.rem(me + hop, tm_size)
+        return pltpu.make_async_remote_copy(
+            src_ref=summed.at[tg, peer],
+            dst_ref=signals.at[me, tg],
+            send_sem=peer_send.at[tg, hop],
+            recv_sem=peer_recv.at[tg, hop],
+            device_id=(peer, core),
+            device_id_type=pl.DeviceIdType.MESH,
+        )
+
+    def reduce_and_send(tg):
+        pair_copy(tg).wait_recv()
+        summed[tg] = modes[tg, core] + from_pair[tg]
+        for hop in range(1, tm_size):
+            peer_copy(tg, hop).start()
+        signals[me, tg] = summed[tg, me]
+
+    row_index = lax.broadcasted_iota(jnp.int32, (256, atoms), 0)
+    for tg in range(groups):
+        rows = []
+        for q in range(4):
+            for spec in (species_a, species_b):
+                if q == 0:
+                    rows.append(jnp.broadcast_to(spec, (GROUP, atoms)))
+                else:
+                    rows.append(vel_ref[q - 1, tg * GROUP : (tg + 1) * GROUP, :] * spec)
+        kinds = jnp.concatenate(rows, 0)
+        high, low = split(kinds)
+        weights[0:128] = high.astype(jnp.float32)
+        weights[128:256] = low.astype(jnp.float32)
+        acc[...] = jnp.zeros_like(acc)
+
+        def step(index, carry):
+            left_cos, left_sin, right = [], [], []
+            for k in range(STEP):
+                local = index * STEP + k
+                cosine, sine = trig(tg * GROUP + local)
+                left_cos += list(split(cosine))
+                left_sin += list(split(sine))
+                frame_w = jnp.where(
+                    (row_index & (GROUP - 1)) == local, weights[...], 0.0
+                ).astype(jnp.bfloat16)
+                right += [frame_w, frame_w]
+            right = jnp.concatenate(right, 1)
+            acc[0:waves] += dot_rows(jnp.concatenate(left_cos, 1), right)
+            acc[waves : 2 * waves] += dot_rows(jnp.concatenate(left_sin, 1), right)
+            return carry
+
+        lax.fori_loop(0, GROUP // STEP, step, 0)
+        halves = []
+        for c in range(2):
+            block = acc[c * waves : (c + 1) * waves]
+            part = (block[:, :128] + block[:, 128:]) * factor[...]
+            current = part + pltpu.roll(part, 96, 1) + pltpu.roll(part, 64, 1)
+            halves.append(jnp.where(lane < 32, part, current))
+        packed = jnp.where(lane < 64, halves[0], pltpu.roll(halves[1], 64, 1))
+        packed = packed.reshape(tm_size, 2, 8, 128)
+        modes[tg, 0] = packed[:, 0]
+        modes[tg, 1] = packed[:, 1]
+        if tg == 0:
+            pl.semaphore_wait(barrier, tm_size)
+        pair_copy(tg).start()
+        reduce_and_send(tg)
+    table_copy.wait()
+    for tg in range(groups):
+        for hop in range(1, tm_size):
+            peer_copy(tg, hop).wait_recv()
+
+    tiles = signals[...].reshape(frame_total // 128, 8, 8, 128)
+    wide = frame_total // 128 * 8
+    group_lane = lax.broadcasted_iota(jnp.int32, (wide, 128), 1) // 16
+    turned = [
+        pltpu.roll(tiles[:, p].reshape(wide, 128), 16 * p, 1) if p else tiles[:, p].reshape(wide, 128)
+        for p in range(8)
+    ]
+    rows = []
+    for m in range(8):
+        picked = turned[0]
+        for p in range(1, 8):
+            picked = jnp.where(group_lane == (m + p) % 8, turned[p], picked)
+        if m:
+            picked = pltpu.roll(picked, 128 - 16 * m, 1)
+        rows.append(
+            jnp.concatenate([picked[v * 8 : v * 8 + 8] for v in range(frame_total // 128)], 1)
+        )
+    high, low = split(jnp.concatenate(rows, 0))
+    both = jnp.dot(
+        jnp.concatenate([high, low], 0), table[0], preferred_element_type=jnp.float32
+    )
+    spectra = both[:64] + both[64:] + jnp.dot(high, table[1], preferred_element_type=jnp.float32)
+    first = lax.broadcasted_iota(jnp.int32, (8, frame_total), 1) == 0
+    out_rows = []
+    for g in range(2):
+        for a, b in ((0, 0), (0, 1), (1, 1)):
+            even = jnp.zeros((8, frame_total), jnp.float32)
+            odd = jnp.zeros((8, frame_total), jnp.float32)
+            imag = jnp.zeros((8, frame_total), jnp.float32)
+            for c in range(2):
+                row_a = (c * 4 + g * 2 + a) * 8
+                row_b = (c * 4 + g * 2 + b) * 8
+                cos_a = spectra[row_a : row_a + 8, :frame_total]
+                sin_a = spectra[row_a : row_a + 8, frame_total:]
+                cos_b = spectra[row_b : row_b + 8, :frame_total]
+                sin_b = spectra[row_b : row_b + 8, frame_total:]
+                even += cos_a * cos_b
+                odd += sin_a * sin_b
+                imag += sin_a * cos_b - cos_a * sin_b
+            real = jnp.where(first, even, 2.0 * (even + odd))
+            imag = jnp.where(first, odd, 2.0 * imag)
+            out_rows.append(jnp.concatenate([real, imag], 1))
+    high, low = split(jnp.concatenate(out_rows, 0))
+    lags = 2 * out_ref.shape[2]
+    both = dot_rows(jnp.concatenate([high, low], 0), table[0, :lags])
+    corr = both[:48] + both[48:] + dot_rows(high, table[1, :lags])
+    lag = lax.broadcasted_iota(jnp.int32, (1, lags), 1)
+    norm = 1.0 / (
+        (frame_total - lag).astype(jnp.float32) * jnp.float32(2 * frame_total * 2 * atoms)
+    )
+    corr = (corr * norm).reshape(6, 8, lags)
+    result[0] = corr[:, :, : lags // 2]
+    result[1] = corr[:, :, lags // 2 :]
+    swap = pltpu.make_async_remote_copy(
+        src_ref=result.at[other],
+        dst_ref=result_in,
+        send_sem=last_send,
+        recv_sem=last_recv,
+        device_id=(me, other),
+        device_id_type=pl.DeviceIdType.MESH,
+    )
+    swap.start()
+    out_ref[:, pl.ds(pl.multiple_of(core * 8, 8), 8), :] = result[core]
+    for tg in range(groups):
+        pair_copy(tg).wait_send()
+        for hop in range(1, tm_size):
+            peer_copy(tg, hop).wait_send()
+    swap.wait()
+    out_ref[:, pl.ds(pl.multiple_of(other * 8, 8), 8), :] = result_in[...]
+
+
+def per_device_fused(tm_size, positions, velocities, species, wave_vectors):
+    frames, atoms = positions.shape[1:]
+    waves = wave_vectors.shape[1]
+    groups = frames // GROUP
+    frame_total = frames * tm_size
+    lag_here = frame_total // 4
+    vmem = pl.BlockSpec(memory_space=pltpu.VMEM)
+    dma = pltpu.SemaphoreType.DMA
+    return pl.pallas_call(
+        lambda *refs: fused_kernel(tm_size, *refs),
+        name="scattering",
+        out_shape=jax.ShapeDtypeStruct((6, 16, lag_here), jnp.float32),
+        in_specs=[vmem] * 4 + [pl.BlockSpec(memory_space=pl.ANY)],
+        out_specs=vmem,
+        scratch_shapes=[
+            pltpu.VMEM((2, frame_total, 2 * frame_total), jnp.bfloat16),
+            pltpu.VMEM((3, waves, 128), jnp.float32),
+            pltpu.VMEM((waves, 128), jnp.float32),
+            pltpu.VMEM((256, atoms), jnp.float32),
+            pltpu.VMEM((2 * waves, 256), jnp.float32),
+            pltpu.VMEM((groups, 2, tm_size, 8, 128), jnp.float32),
+            pltpu.VMEM((groups, tm_size, 8, 128), jnp.float32),
+            pltpu.VMEM((groups, tm_size, 8, 128), jnp.float32),
+            pltpu.VMEM((tm_size, groups, 8, 128), jnp.float32),
+            pltpu.VMEM((2, 6, 8, lag_here), jnp.float32),
+            pltpu.VMEM((6, 8, lag_here), jnp.float32),
+            dma,
+            dma((groups,)),
+            dma((groups,)),
+            dma((groups, tm_size)),
+            dma((groups, tm_size)),
+            dma,
+            dma,
+        ],
+        compiler_params=pltpu.CompilerParams(
+            collective_id=0, has_side_effects=True, vmem_limit_bytes=48 << 20
+        ),
+    )(
+        positions,
+        velocities,
+        species.reshape(1, atoms),
+        wave_vectors,
+        jnp.asarray(dft_tables(frame_total)),
+    )
+
+
 def solution(mesh):
+    tm_size = mesh.shape["tm"]
+    atom_size = mesh.shape["atom"]
+
+    def per_device(positions, velocities, species, wave_vectors):
+        frames, atoms = positions.shape[1:]
+        waves = wave_vectors.shape[1]
+        fits = (
+            tm_size == 16
+            and atom_size == 2
+            and frames == 2 * GROUP
+            and atoms == 256
+            and waves == 256
+        )
+        if fits:
+            return per_device_fused(tm_size, positions, velocities, species, wave_vectors)
+        return per_device_general(positions, velocities, species, wave_vectors)
+
     return jax.shard_map(
         per_device,
         mesh=mesh,

time: 161 us -> 32.6 us (0.20)
  matrix products: 88.1 us -> 0 us
  waiting for transfers between devices: 36.8 us -> 0 us
  Pallas kernels: 0 us -> 27 us
  between operations: 13.6 us -> 0.01 us
  starting transfers between devices: 7.01 us -> 0 us
  other arithmetic: 4.92 us -> 0 us
  local copies, waits for them, and re-layouts: 8.99 us -> 5.36 us
    dot_general x37 -> x0, matrix products: 88.1 us -> none  [the longest x16 39.8 us: frame_block(): jnp.einsum('qsba,bak->qsbk', weights, jnp.sin(phase), precision=highest)]
    pallas_call x0 -> x1, Pallas kernels: none -> 27 us  [per_device_fused(): pl.pallas_call(lambda *refs: fused_kernel(tm_size, *refs), name='scatteri...]
    psum x1 -> x0, waiting for transfers between devices: 21.1 us -> none  [per_device(): summed = lax.psum(modes, 'atom')]
    all_to_all x1 -> x0, waiting for transfers between devices: 10 us -> none  [per_device(): lax.all_to_all(summed, 'tm', split_axis=4, concat_axis=3, tiled=True)]
    all_to_all x1 -> x0, starting transfers between devices: 6.78 us -> none  [per_device(): lax.all_to_all(summed, 'tm', split_axis=4, concat_axis=3, tiled=True)]
    reduce_scatter x1 -> x0, waiting for transfers between devices: 5.55 us -> none  [correlate(): lax.psum_scatter(term + lag_sign[:, None] * nyq_here[None, :], 'atom', sc...]
    div x2 -> x0, other arithmetic: 2.12 us -> none  [the longest x1 1.43 us: correlate(): scaled / (jnp.float32(atom_total) * (frame_total - lag_index).astype(jnp....]
    psum x1 -> x0, local copies, waits for them, and re-layouts: 1.61 us -> none  [per_device(): summed = lax.psum(modes, 'atom')]
  transfers between devices with their start and end apart: 3 -> 0, of which waited for: 3 -> 0; matrix products, arithmetic and copies ran while one was open for 0% -> 0% of each run, Pallas kernels for 0% -> 0%
where the time goes in v1:
time: 32.6 us; the launch traced here: 32.3 us
  Pallas kernels  27 us (83%)
  local copies, waits for them, and re-layouts  5.36 us (16%)
    pallas_call x1, Pallas kernels, per_device_fused(): pl.pallas_call(lambda *refs: fused_kernel(tm_size, *refs), name='scatteri...  27 us
    unnamed x11, local copies, waits for them, and re-layouts  5.36 us

profile of v1, /device:TPU:0, one launch (start us, length us, event | category | flops | bytes accessed | tf_op | source)
XLA Modules:
  0.0 32.3 jit_solution(13519177312259529416)
XLA Ops:
  0.0 0.0 copy-start
  0.0 1.6 %copy-done = bf16[2,512,1024]{2,1,0:T(8,128)(2,1)S(1)} copy-done((bf16[2,512,1024]{2,1,0:T(8,128)(2,1)S(1)}, bf16[2,512,1024]{2,1,0:T(8,128)(2,1)}, u32[]{:S(2)}) %copy-start) | copy-done | bytes 2097176
  1.6 0.0 copy-start.1
  1.6 0.9 %copy-done.1 = s32[3,32,256]{2,1,0:T(8,128)S(1)} copy-done((s32[3,32,256]{2,1,0:T(8,128)S(1)}, s32[3,32,256]{2,1,0:T(8,128)}, u32[]{:S(2)}) %copy-start.1) | copy-done | bytes 98328
  2.5 0.0 copy-start.2
  2.5 0.9 %copy-done.2 = f32[3,32,256]{2,1,0:T(8,128)S(1)} copy-done((f32[3,32,256]{2,1,0:T(8,128)S(1)}, f32[3,32,256]{2,1,0:T(8,128)}, u32[]{:S(2)}) %copy-start.2) | copy-done | bytes 98328
  3.4 0.0 copy-start.3
  3.4 0.7 %copy-done.3 = s32[3,256]{1,0:T(4,128)S(1)} copy-done((s32[3,256]{1,0:T(4,128)S(1)}, s32[3,256]{1,0:T(4,128)}, u32[]{:S(2)}) %copy-start.3) | copy-done | bytes 3096
  4.1 0.0 copy-start.4
  4.1 0.7 %copy-done.4 = s32[256]{0:T(256)S(1)} copy-done((s32[256]{0:T(256)S(1)}, s32[256]{0:T(256)}, u32[]{:S(2)}) %copy-start.4) | copy-done | bytes 1048
  4.7 27.0 %scattering.1 = f32[6,16,128]{2,1,0:T(8,128)S(1)} custom-call(s32[3,32,256]{2,1,0:T(8,128)S(1)} %copy-done.1, f32[3,32,256]{2,1,0:T(8,128)S(1)} %copy-done.2, s32[1,256]{1,0:T(1,128)S(1)} %bitcast.1, s32[3,256]{1,0:T(4,128)S(1)} %copy-done.3, bf16[2,512,1024]{2,1,0:T(8,128)(2,1)S(1)} %copy-done), custom_call_target="tpu_custom_call" | custom-call | tf_op jit(solution)/shard_map/scattering/pallas_call | solution.py:408
  31.7 0.6 %copy.7 = f32[6,16,128]{2,1,0:T(8,128)} copy(f32[6,16,128]{2,1,0:T(8,128)S(1)} %scattering.1) | data formatting | bytes 98304
Async XLA Ops:
  0.0 1.6 %copy-start = (bf16[2,512,1024]{2,1,0:T(8,128)(2,1)S(1)}, bf16[2,512,1024]{2,1,0:T(8,128)(2,1)}, u32[]{:S(2)}) copy-start(bf16[2,512,1024]{2,1,0:T(8,128)(2,1)} %constant.2.clone.refs_4_) | copy-start | bytes 6291460
  1.6 0.9 %copy-start.1 = (s32[3,32,256]{2,1,0:T(8,128)S(1)}, s32[3,32,256]{2,1,0:T(8,128)}, u32[]{:S(2)}) copy-start(s32[3,32,256]{2,1,0:T(8,128)} %refs_0_.1) | copy-start | bytes 294916
  2.5 0.9 %copy-start.2 = (f32[3,32,256]{2,1,0:T(8,128)S(1)}, f32[3,32,256]{2,1,0:T(8,128)}, u32[]{:S(2)}) copy-start(f32[3,32,256]{2,1,0:T(8,128)} %refs_1_.1) | copy-start | bytes 294916
  3.4 0.7 %copy-start.3 = (s32[3,256]{1,0:T(4,128)S(1)}, s32[3,256]{1,0:T(4,128)}, u32[]{:S(2)}) copy-start(s32[3,256]{1,0:T(4,128)} %refs_3_.1) | copy-start | bytes 9220
  4.1 0.7 %copy-start.4 = (s32[256]{0:T(256)S(1)}, s32[256]{0:T(256)}, u32[]{:S(2)}) copy-start(s32[256]{0:T(256)} %param.7) | copy-start | bytes 3076

commit v2 on v1

--- a/solution.py
+++ b/solution.py
@@ -132,7 +132,7 @@
 
 
 GROUP = 16
-STEP = 2
+STEP = 4
 
 
 def even_coeffs(func, degree):
@@ -142,8 +142,8 @@
     return [float(v) for v in fit.convert(kind=np.polynomial.Polynomial).coef]
 
 
-COS_COEFFS = even_coeffs(lambda r: np.cos(2 * np.pi * r), 5)
-SIN_COEFFS = even_coeffs(lambda r: np.sin(2 * np.pi * r) / r, 4)
+COS_COEFFS = even_coeffs(lambda r: np.sqrt(2.0) * np.cos(np.pi * r), 3)
+SIN_COEFFS = even_coeffs(lambda r: np.sqrt(2.0) * np.sin(np.pi * r) / r, 3)
 
 
 def dft_tables(frames):
@@ -178,12 +178,16 @@
 
 def fused_kernel(
     tm_size,
+    pos_hbm,
+    vel_hbm,
+    species_hbm,
+    wave_hbm,
+    table_hbm,
+    out_ref,
     pos_ref,
     vel_ref,
     species_ref,
     wave_ref,
-    table_hbm,
-    out_ref,
     table,
     wave_cols,
     factor,
@@ -195,7 +199,7 @@
     signals,
     result,
     result_in,
-    table_sem,
+    load_sem,
     pair_send,
     pair_recv,
     peer_send,
@@ -211,7 +215,22 @@
     atoms = pos_ref.shape[2]
     groups = frames // GROUP
     frame_total = frames * tm_size
-
+    early = GROUP // STEP // 2
+
+    loads = [
+        pltpu.make_async_copy(source, target, load_sem.at[n])
+        for n, (source, target) in enumerate(
+            (
+                (wave_hbm, wave_ref),
+                (species_hbm, species_ref),
+                (vel_hbm, vel_ref),
+                (pos_hbm, pos_ref),
+                (table_hbm, table),
+            )
+        )
+    ]
+    for load in loads:
+        load.start()
     barrier = pltpu.get_barrier_semaphore()
     for hop in range(1, tm_size):
         peer = lax.rem(me + hop, tm_size)
@@ -221,9 +240,8 @@
     pl.semaphore_signal(
         barrier, inc=1, device_id=(me, other), device_id_type=pl.DeviceIdType.MESH
     )
-    table_copy = pltpu.make_async_copy(table_hbm, table, table_sem)
-    table_copy.start()
-
+
+    loads[0].wait()
     lane = lax.broadcasted_iota(jnp.int32, (waves, 128), 1)
     for d in range(3):
         row = wave_ref[d : d + 1, :].astype(jnp.float32)
@@ -232,6 +250,8 @@
         lane < 64, wave_cols[0], jnp.where(lane < 96, wave_cols[1], wave_cols[2])
     ) * (1.0 / WAVE_MAX)
     factor[...] = jnp.where(lane < 32, 1.0, scaled)
+    for load in loads[1:4]:
+        load.wait()
     species_b = species_ref[...].astype(jnp.float32)
     species_a = 1.0 - species_b
 
@@ -245,7 +265,8 @@
         magic = jnp.float32(12582912.0)
         rest = turn - ((turn + magic) - magic)
         z = rest * rest
-        return horner(COS_COEFFS, z), rest * horner(SIN_COEFFS, z)
+        half_sin = rest * horner(SIN_COEFFS, z)
+        return 1.0 - half_sin * half_sin, half_sin * horner(COS_COEFFS, z)
 
     def pair_copy(tg):
         return pltpu.make_async_remote_copy(
@@ -306,7 +327,12 @@
             acc[waves : 2 * waves] += dot_rows(jnp.concatenate(left_sin, 1), right)
             return carry
 
-        lax.fori_loop(0, GROUP // STEP, step, 0)
+        if tg > 0:
+            lax.fori_loop(0, early, step, 0)
+            reduce_and_send(tg - 1)
+            lax.fori_loop(early, GROUP // STEP, step, 0)
+        else:
+            lax.fori_loop(0, GROUP // STEP, step, 0)
         halves = []
         for c in range(2):
             block = acc[c * waves : (c + 1) * waves]
@@ -320,8 +346,8 @@
         if tg == 0:
             pl.semaphore_wait(barrier, tm_size)
         pair_copy(tg).start()
-        reduce_and_send(tg)
-    table_copy.wait()
+    reduce_and_send(groups - 1)
+    loads[4].wait()
     for tg in range(groups):
         for hop in range(1, tm_size):
             peer_copy(tg, hop).wait_recv()
@@ -409,9 +435,13 @@
         lambda *refs: fused_kernel(tm_size, *refs),
         name="scattering",
         out_shape=jax.ShapeDtypeStruct((6, 16, lag_here), jnp.float32),
-        in_specs=[vmem] * 4 + [pl.BlockSpec(memory_space=pl.ANY)],
+        in_specs=[pl.BlockSpec(memory_space=pltpu.HBM)] * 5,
         out_specs=vmem,
         scratch_shapes=[
+            pltpu.VMEM(positions.shape, jnp.int32),
+            pltpu.VMEM(velocities.shape, jnp.float32),
+            pltpu.VMEM((1, atoms), jnp.int32),
+            pltpu.VMEM(wave_vectors.shape, jnp.int32),
             pltpu.VMEM((2, frame_total, 2 * frame_total), jnp.bfloat16),
             pltpu.VMEM((3, waves, 128), jnp.float32),
             pltpu.VMEM((waves, 128), jnp.float32),
@@ -423,7 +453,7 @@
             pltpu.VMEM((tm_size, groups, 8, 128), jnp.float32),
             pltpu.VMEM((2, 6, 8, lag_here), jnp.float32),
             pltpu.VMEM((6, 8, lag_here), jnp.float32),
-            dma,
+            dma((5,)),
             dma((groups,)),
             dma((groups,)),
             dma((groups, tm_size)),

time: 32.6 us -> 29.3 us (0.90)
  Pallas kernels: 27 us -> 23.7 us
    pallas_call x1, Pallas kernels: 27 us -> 23.7 us  [per_device_fused(): pl.pallas_call(lambda *refs: fused_kernel(tm_size, *refs), name='scatteri...]
where the time goes in v2:
time: 29.3 us; the launch traced here: 29.1 us
  Pallas kernels  23.7 us (81%)
  local copies, waits for them, and re-layouts  5.36 us (18%)
    pallas_call x1, Pallas kernels, per_device_fused(): pl.pallas_call(lambda *refs: fused_kernel(tm_size, *refs), name='scatteri...  23.7 us
    unnamed x11, local copies, waits for them, and re-layouts  5.36 us

profile of v2, /device:TPU:0, one launch (start us, length us, event | category | flops | bytes accessed | tf_op | source)
XLA Modules:
  0.0 29.1 jit_solution(8283753388927924795)
XLA Ops:
  0.0 0.0 copy-start
  0.0 1.6 %copy-done = bf16[2,512,1024]{2,1,0:T(8,128)(2,1)S(1)} copy-done((bf16[2,512,1024]{2,1,0:T(8,128)(2,1)S(1)}, bf16[2,512,1024]{2,1,0:T(8,128)(2,1)}, u32[]{:S(2)}) %copy-start) | copy-done | bytes 2097176
  1.6 0.0 copy-start.1
  1.6 0.9 %copy-done.1 = s32[3,32,256]{2,1,0:T(8,128)S(1)} copy-done((s32[3,32,256]{2,1,0:T(8,128)S(1)}, s32[3,32,256]{2,1,0:T(8,128)}, u32[]{:S(2)}) %copy-start.1) | copy-done | bytes 98328
  2.5 0.0 copy-start.2
  2.5 0.9 %copy-done.2 = f32[3,32,256]{2,1,0:T(8,128)S(1)} copy-done((f32[3,32,256]{2,1,0:T(8,128)S(1)}, f32[3,32,256]{2,1,0:T(8,128)}, u32[]{:S(2)}) %copy-start.2) | copy-done | bytes 98328
  3.4 0.0 copy-start.3
  3.4 0.7 %copy-done.3 = s32[3,256]{1,0:T(4,128)S(1)} copy-done((s32[3,256]{1,0:T(4,128)S(1)}, s32[3,256]{1,0:T(4,128)}, u32[]{:S(2)}) %copy-start.3) | copy-done | bytes 3096
  4.1 0.0 copy-start.4
  4.1 0.7 %copy-done.4 = s32[256]{0:T(256)S(1)} copy-done((s32[256]{0:T(256)S(1)}, s32[256]{0:T(256)}, u32[]{:S(2)}) %copy-start.4) | copy-done | bytes 1048
  4.7 23.7 %scattering.1 = f32[6,16,128]{2,1,0:T(8,128)S(1)} custom-call(s32[3,32,256]{2,1,0:T(8,128)S(1)} %copy-done.1, f32[3,32,256]{2,1,0:T(8,128)S(1)} %copy-done.2, s32[1,256]{1,0:T(1,128)S(1)} %bitcast.1, s32[3,256]{1,0:T(4,128)S(1)} %copy-done.3, bf16[2,512,1024]{2,1,0:T(8,128)(2,1)S(1)} %copy-done), custom_call_target="tpu_custom_call" | custom-call | tf_op jit(solution)/shard_map/scattering/pallas_call | solution.py:434
  28.4 0.6 %copy.7 = f32[6,16,128]{2,1,0:T(8,128)} copy(f32[6,16,128]{2,1,0:T(8,128)S(1)} %scattering.1) | data formatting | bytes 98304
Async XLA Ops:
  0.0 1.6 %copy-start = (bf16[2,512,1024]{2,1,0:T(8,128)(2,1)S(1)}, bf16[2,512,1024]{2,1,0:T(8,128)(2,1)}, u32[]{:S(2)}) copy-start(bf16[2,512,1024]{2,1,0:T(8,128)(2,1)} %constant.2.clone.refs_4_) | copy-start | bytes 6291460
  1.6 0.9 %copy-start.1 = (s32[3,32,256]{2,1,0:T(8,128)S(1)}, s32[3,32,256]{2,1,0:T(8,128)}, u32[]{:S(2)}) copy-start(s32[3,32,256]{2,1,0:T(8,128)} %refs_0_.1) | copy-start | bytes 294916
  2.5 0.9 %copy-start.2 = (f32[3,32,256]{2,1,0:T(8,128)S(1)}, f32[3,32,256]{2,1,0:T(8,128)}, u32[]{:S(2)}) copy-start(f32[3,32,256]{2,1,0:T(8,128)} %refs_1_.1) | copy-start | bytes 294916
  3.4 0.7 %copy-start.3 = (s32[3,256]{1,0:T(4,128)S(1)}, s32[3,256]{1,0:T(4,128)}, u32[]{:S(2)}) copy-start(s32[3,256]{1,0:T(4,128)} %refs_3_.1) | copy-start | bytes 9220
  4.1 0.7 %copy-start.4 = (s32[256]{0:T(256)S(1)}, s32[256]{0:T(256)}, u32[]{:S(2)}) copy-start(s32[256]{0:T(256)} %param.7) | copy-start | bytes 3076

commit v3 on v2

--- a/solution.py
+++ b/solution.py
@@ -132,7 +132,7 @@
 
 
 GROUP = 16
-STEP = 4
+STEP = 8
 
 
 def even_coeffs(func, degree):
@@ -297,14 +297,14 @@
         signals[me, tg] = summed[tg, me]
 
     row_index = lax.broadcasted_iota(jnp.int32, (256, atoms), 0)
-    for tg in range(groups):
+    def group(tg, carry):
         rows = []
         for q in range(4):
             for spec in (species_a, species_b):
                 if q == 0:
                     rows.append(jnp.broadcast_to(spec, (GROUP, atoms)))
                 else:
-                    rows.append(vel_ref[q - 1, tg * GROUP : (tg + 1) * GROUP, :] * spec)
+                    rows.append(vel_ref[q - 1, pl.ds(pl.multiple_of(tg * GROUP, GROUP), GROUP), :] * spec)
         kinds = jnp.concatenate(rows, 0)
         high, low = split(kinds)
         weights[0:128] = high.astype(jnp.float32)
@@ -312,6 +312,14 @@
         acc[...] = jnp.zeros_like(acc)
 
         def step(index, carry):
+            @pl.when(jnp.logical_and(tg == 0, index == GROUP // STEP - 1))
+            def _():
+                pl.semaphore_wait(barrier, tm_size)
+
+            @pl.when(jnp.logical_and(tg > 0, index == early))
+            def _():
+                reduce_and_send(tg - 1)
+
             left_cos, left_sin, right = [], [], []
             for k in range(STEP):
                 local = index * STEP + k
@@ -327,12 +335,7 @@
             acc[waves : 2 * waves] += dot_rows(jnp.concatenate(left_sin, 1), right)
             return carry
 
-        if tg > 0:
-            lax.fori_loop(0, early, step, 0)
-            reduce_and_send(tg - 1)
-            lax.fori_loop(early, GROUP // STEP, step, 0)
-        else:
-            lax.fori_loop(0, GROUP // STEP, step, 0)
+        lax.fori_loop(0, GROUP // STEP, step, 0)
         halves = []
         for c in range(2):
             block = acc[c * waves : (c + 1) * waves]
@@ -343,9 +346,10 @@
         packed = packed.reshape(tm_size, 2, 8, 128)
         modes[tg, 0] = packed[:, 0]
         modes[tg, 1] = packed[:, 1]
-        if tg == 0:
-            pl.semaphore_wait(barrier, tm_size)
         pair_copy(tg).start()
+        return carry
+
+    lax.fori_loop(0, groups, group, 0)
     reduce_and_send(groups - 1)
     loads[4].wait()
     for tg in range(groups):

time: 29.3 us -> 28.7 us (0.980)
  Pallas kernels: 23.7 us -> 23.1 us
    pallas_call x1, Pallas kernels: 23.7 us -> 23.1 us  [per_device_fused(): pl.pallas_call(lambda *refs: fused_kernel(tm_size, *refs), name='scatteri...]
where the time goes in v3:
time: 28.7 us; the launch traced here: 28.5 us
  Pallas kernels  23.1 us (80%)
  local copies, waits for them, and re-layouts  5.36 us (19%)
    pallas_call x1, Pallas kernels, per_device_fused(): pl.pallas_call(lambda *refs: fused_kernel(tm_size, *refs), name='scatteri...  23.1 us
    unnamed x11, local copies, waits for them, and re-layouts  5.36 us

profile of v3, /device:TPU:0, one launch (start us, length us, event | category | flops | bytes accessed | tf_op | source)
XLA Modules:
  0.0 28.5 jit_solution(9975628368979916584)
XLA Ops:
  0.0 0.0 copy-start
  0.0 1.6 %copy-done = bf16[2,512,1024]{2,1,0:T(8,128)(2,1)S(1)} copy-done((bf16[2,512,1024]{2,1,0:T(8,128)(2,1)S(1)}, bf16[2,512,1024]{2,1,0:T(8,128)(2,1)}, u32[]{:S(2)}) %copy-start) | copy-done | bytes 2097176
  1.6 0.0 copy-start.1
  1.6 0.9 %copy-done.1 = s32[3,32,256]{2,1,0:T(8,128)S(1)} copy-done((s32[3,32,256]{2,1,0:T(8,128)S(1)}, s32[3,32,256]{2,1,0:T(8,128)}, u32[]{:S(2)}) %copy-start.1) | copy-done | bytes 98328
  2.5 0.0 copy-start.2
  2.5 0.9 %copy-done.2 = f32[3,32,256]{2,1,0:T(8,128)S(1)} copy-done((f32[3,32,256]{2,1,0:T(8,128)S(1)}, f32[3,32,256]{2,1,0:T(8,128)}, u32[]{:S(2)}) %copy-start.2) | copy-done | bytes 98328
  3.4 0.0 copy-start.3
  3.4 0.7 %copy-done.3 = s32[3,256]{1,0:T(4,128)S(1)} copy-done((s32[3,256]{1,0:T(4,128)S(1)}, s32[3,256]{1,0:T(4,128)}, u32[]{:S(2)}) %copy-start.3) | copy-done | bytes 3096
  4.1 0.0 copy-start.4
  4.1 0.7 %copy-done.4 = s32[256]{0:T(256)S(1)} copy-done((s32[256]{0:T(256)S(1)}, s32[256]{0:T(256)}, u32[]{:S(2)}) %copy-start.4) | copy-done | bytes 1048
  4.7 23.1 %scattering.1 = f32[6,16,128]{2,1,0:T(8,128)S(1)} custom-call(s32[3,32,256]{2,1,0:T(8,128)S(1)} %copy-done.1, f32[3,32,256]{2,1,0:T(8,128)S(1)} %copy-done.2, s32[1,256]{1,0:T(1,128)S(1)} %bitcast.1, s32[3,256]{1,0:T(4,128)S(1)} %copy-done.3, bf16[2,512,1024]{2,1,0:T(8,128)(2,1)S(1)} %copy-done), custom_call_target="tpu_custom_call" | custom-call | tf_op jit(solution)/shard_map/scattering/pallas_call | solution.py:438
  27.9 0.6 %copy.7 = f32[6,16,128]{2,1,0:T(8,128)} copy(f32[6,16,128]{2,1,0:T(8,128)S(1)} %scattering.1) | data formatting | bytes 98304
Async XLA Ops:
  0.0 1.6 %copy-start = (bf16[2,512,1024]{2,1,0:T(8,128)(2,1)S(1)}, bf16[2,512,1024]{2,1,0:T(8,128)(2,1)}, u32[]{:S(2)}) copy-start(bf16[2,512,1024]{2,1,0:T(8,128)(2,1)} %constant.2.clone.refs_4_) | copy-start | bytes 6291460
  1.6 0.9 %copy-start.1 = (s32[3,32,256]{2,1,0:T(8,128)S(1)}, s32[3,32,256]{2,1,0:T(8,128)}, u32[]{:S(2)}) copy-start(s32[3,32,256]{2,1,0:T(8,128)} %refs_0_.1) | copy-start | bytes 294916
  2.5 0.9 %copy-start.2 = (f32[3,32,256]{2,1,0:T(8,128)S(1)}, f32[3,32,256]{2,1,0:T(8,128)}, u32[]{:S(2)}) copy-start(f32[3,32,256]{2,1,0:T(8,128)} %refs_1_.1) | copy-start | bytes 294916
  3.4 0.7 %copy-start.3 = (s32[3,256]{1,0:T(4,128)S(1)}, s32[3,256]{1,0:T(4,128)}, u32[]{:S(2)}) copy-start(s32[3,256]{1,0:T(4,128)} %refs_3_.1) | copy-start | bytes 9220
  4.1 0.7 %copy-start.4 = (s32[256]{0:T(256)S(1)}, s32[256]{0:T(256)}, u32[]{:S(2)}) copy-start(s32[256]{0:T(256)} %param.7) | copy-start | bytes 3076

commit v4 on v3

--- a/solution.py
+++ b/solution.py
@@ -262,8 +262,7 @@
             wave = wave_cols[d]
             term = jnp.concatenate([wave] * (atoms // 128), 1) * coord
             turn = term if turn is None else turn + term
-        magic = jnp.float32(12582912.0)
-        rest = turn - ((turn + magic) - magic)
+        rest = turn - jnp.round(turn)
         z = rest * rest
         half_sin = rest * horner(SIN_COEFFS, z)
         return 1.0 - half_sin * half_sin, half_sin * horner(COS_COEFFS, z)

time: 28.7 us -> 28.5 us (level)
  Pallas kernels: 23.1 us -> 22.8 us
where the time goes in v4:
time: 28.5 us; the launch traced here: 28.2 us
  Pallas kernels  22.8 us (80%)
  local copies, waits for them, and re-layouts  5.36 us (19%)
    pallas_call x1, Pallas kernels, per_device_fused(): pl.pallas_call(lambda *refs: fused_kernel(tm_size, *refs), name='scatteri...  22.8 us
    unnamed x11, local copies, waits for them, and re-layouts  5.36 us

profile of v4, /device:TPU:0, one launch (start us, length us, event | category | flops | bytes accessed | tf_op | source)
XLA Modules:
  0.0 28.2 jit_solution(5922790687034160492)
XLA Ops:
  0.0 0.0 copy-start
  0.0 1.6 %copy-done = bf16[2,512,1024]{2,1,0:T(8,128)(2,1)S(1)} copy-done((bf16[2,512,1024]{2,1,0:T(8,128)(2,1)S(1)}, bf16[2,512,1024]{2,1,0:T(8,128)(2,1)}, u32[]{:S(2)}) %copy-start) | copy-done | bytes 2097176
  1.6 0.0 copy-start.1
  1.6 0.9 %copy-done.1 = s32[3,32,256]{2,1,0:T(8,128)S(1)} copy-done((s32[3,32,256]{2,1,0:T(8,128)S(1)}, s32[3,32,256]{2,1,0:T(8,128)}, u32[]{:S(2)}) %copy-start.1) | copy-done | bytes 98328
  2.5 0.0 copy-start.2
  2.5 0.9 %copy-done.2 = f32[3,32,256]{2,1,0:T(8,128)S(1)} copy-done((f32[3,32,256]{2,1,0:T(8,128)S(1)}, f32[3,32,256]{2,1,0:T(8,128)}, u32[]{:S(2)}) %copy-start.2) | copy-done | bytes 98328
  3.4 0.0 copy-start.3
  3.4 0.7 %copy-done.3 = s32[3,256]{1,0:T(4,128)S(1)} copy-done((s32[3,256]{1,0:T(4,128)S(1)}, s32[3,256]{1,0:T(4,128)}, u32[]{:S(2)}) %copy-start.3) | copy-done | bytes 3096
  4.1 0.0 copy-start.4
  4.1 0.7 %copy-done.4 = s32[256]{0:T(256)S(1)} copy-done((s32[256]{0:T(256)S(1)}, s32[256]{0:T(256)}, u32[]{:S(2)}) %copy-start.4) | copy-done | bytes 1048
  4.7 22.8 %scattering.1 = f32[6,16,128]{2,1,0:T(8,128)S(1)} custom-call(s32[3,32,256]{2,1,0:T(8,128)S(1)} %copy-done.1, f32[3,32,256]{2,1,0:T(8,128)S(1)} %copy-done.2, s32[1,256]{1,0:T(1,128)S(1)} %bitcast.1, s32[3,256]{1,0:T(4,128)S(1)} %copy-done.3, bf16[2,512,1024]{2,1,0:T(8,128)(2,1)S(1)} %copy-done), custom_call_target="tpu_custom_call" | custom-call | tf_op jit(solution)/shard_map/scattering/pallas_call | solution.py:437
  27.6 0.6 %copy.7 = f32[6,16,128]{2,1,0:T(8,128)} copy(f32[6,16,128]{2,1,0:T(8,128)S(1)} %scattering.1) | data formatting | bytes 98304
Async XLA Ops:
  0.0 1.6 %copy-start = (bf16[2,512,1024]{2,1,0:T(8,128)(2,1)S(1)}, bf16[2,512,1024]{2,1,0:T(8,128)(2,1)}, u32[]{:S(2)}) copy-start(bf16[2,512,1024]{2,1,0:T(8,128)(2,1)} %constant.2.clone.refs_4_) | copy-start | bytes 6291460
  1.6 0.9 %copy-start.1 = (s32[3,32,256]{2,1,0:T(8,128)S(1)}, s32[3,32,256]{2,1,0:T(8,128)}, u32[]{:S(2)}) copy-start(s32[3,32,256]{2,1,0:T(8,128)} %refs_0_.1) | copy-start | bytes 294916
  2.5 0.9 %copy-start.2 = (f32[3,32,256]{2,1,0:T(8,128)S(1)}, f32[3,32,256]{2,1,0:T(8,128)}, u32[]{:S(2)}) copy-start(f32[3,32,256]{2,1,0:T(8,128)} %refs_1_.1) | copy-start | bytes 294916
  3.4 0.7 %copy-start.3 = (s32[3,256]{1,0:T(4,128)S(1)}, s32[3,256]{1,0:T(4,128)}, u32[]{:S(2)}) copy-start(s32[3,256]{1,0:T(4,128)} %refs_3_.1) | copy-start | bytes 9220
  4.1 0.7 %copy-start.4 = (s32[256]{0:T(256)S(1)}, s32[256]{0:T(256)}, u32[]{:S(2)}) copy-start(s32[256]{0:T(256)} %param.7) | copy-start | bytes 3076
